TPU v7x, 512 devices: a whole 4x8x8 slice. The times are simulated.
512 devices in a mesh: outer: 2 (over core), row: 256 (over y, z, x).
Axes of the slice: x: 4, y: 8, z: 8, core: 2. Of those that a mesh axis runs over, the one named last changes fastest.
Arguments:
- grad_gate: bfloat16 [2, 8192, 14336], P('outer', 'row'), may hold values from -24 to 24
- grad_up: bfloat16 [2, 8192, 14336], P('outer', 'row'), may hold values from -24 to 24
- basis_gate: bfloat16 [32, 14336], P(None, 'row'), may hold values from -0.046875 to 0.046875
- basis_up: bfloat16 [32, 14336], P(None, 'row'), may hold values from -0.046875 to 0.046875
Outputs:
- next_gate: float32 [32, 14336], P(None, 'row')
- next_up: float32 [32, 14336], P(None, 'row')
- factor_gate: float32 [8192, 32], P('row')
- factor_up: float32 [8192, 32], P('row')
- resid_gate: bfloat16 [2, 8192, 14336], P('outer', 'row')
- resid_up: bfloat16 [2, 8192, 14336], P('outer', 'row')
All inputs are finite; a program needn't handle non-finite values.
Results may differ from a plain program's by a relative error of at most 0.005.
Values may be sent and summed in bfloat16 or wider, within the bound.
No kernel may reach another device: no remote copies, remote signals or barrier semaphores. Data moves between devices by JAX's collectives and lax.ppermute only.
A program may use at most 64 MiB of HBM per device.

v0:
```python
import jax
import jax.numpy as jnp
from jax import lax
from jax.sharding import Mesh
from jax.sharding import PartitionSpec as P

ROW = ("row_0", "row_1", "row_2")
OUTER_ROW = ("outer", "row_0", "row_1", "row_2")


def gather_turned(arrays, axis, dims):
    turned = [jnp.moveaxis(a, dim, 0) for a, dim in zip(arrays, dims)]
    widths = [t[0].size for t in turned]
    both = jnp.concatenate([t.reshape(-1, w) for t, w in zip(turned, widths)], axis=1)
    out = lax.all_gather(both, axis, axis=0, tiled=True)
    tiles = jnp.split(out, [sum(widths[:k]) for k in range(1, len(widths))], axis=1)
    return tuple(
        (
            jnp.moveaxis(b.reshape(-1, *t.shape[1:]), 0, dim)
            for b, t, dim in zip(tiles, turned, dims)
        )
    )


def copy_for_each(x, axis):
    peers = lax.axis_size(axis)
    return lax.all_to_all(jnp.broadcast_to(x[None], (peers, *x.shape)), axis, 0, 0, tiled=True)


def taken_together(x, axis):
    everything = copy_for_each(x, axis)
    return jnp.sum(everything, axis=0)


def together(arrays, axis):
    line, at, finished = (jnp.concatenate([a.reshape(-1) for a in arrays]), 0, [])
    so_far = taken_together(line, axis)
    for a in arrays:
        finished.append(so_far[at : at + a.size].reshape(a.shape))
        at += a.size
    return tuple(finished)


def over_axes(x, axes):
    for axis in axes:
        x = lax.psum(x, axis)
    return x


def forward_solve(lower_matrix, right_hand):
    return jax.scipy.linalg.solve_triangular(lower_matrix, right_hand, lower=True)


def contract_cols(left, right):
    return lax.dot_general(
        left, right, (((1,), (1,)), ((), ())), preferred_element_type=jnp.float32
    )


def contract_rows(left, right):
    return lax.dot_general(
        left, right, (((0,), (0,)), ((), ())), preferred_element_type=jnp.float32
    )


def local(grad_gate, grad_up, basis_gate, basis_up):
    pod_count = lax.axis_size("outer")
    gate_rows = grad_gate[0]
    up_rows = grad_up[0]
    full_cols = gate_rows.shape[1]
    pieces = gather_turned((basis_gate, basis_up), ROW, (1, 1))
    summed = together(
        (contract_cols(gate_rows, pieces[0]), contract_cols(up_rows, pieces[1])), "outer"
    )
    round_gate = (summed[0] / pod_count).astype(jnp.bfloat16)
    round_up = (summed[1] / pod_count).astype(jnp.bfloat16)
    gram_pair = (
        over_axes(contract_rows(round_gate, round_gate), ROW),
        over_axes(contract_rows(round_up, round_up), ROW),
    )
    lower_gate = jnp.linalg.cholesky(gram_pair[0])
    lower_up = jnp.linalg.cholesky(gram_pair[1])
    products = (contract_rows(round_gate, gate_rows), contract_rows(round_up, up_rows))
    shard_cols = full_cols // lax.axis_size(ROW)
    shard_start = lax.axis_index(ROW) * shard_cols
    totals = lax.psum((products[0], products[1]), OUTER_ROW)
    full_gate = forward_solve(lower_gate, totals[0] / pod_count)
    full_up = forward_solve(lower_up, totals[1] / pod_count)
    next_gate = lax.dynamic_slice_in_dim(full_gate, shard_start, shard_cols, 1)
    next_up = lax.dynamic_slice_in_dim(full_up, shard_start, shard_cols, 1)
    factor_gate = forward_solve(lower_gate, round_gate.astype(jnp.float32).T).T
    factor_up = forward_solve(lower_up, round_up.astype(jnp.float32).T).T
    resid_gate = (
        gate_rows - jnp.dot(factor_gate, full_gate, precision=lax.Precision.HIGHEST)
    ).astype(jnp.bfloat16)
    resid_up = (up_rows - jnp.dot(factor_up, full_up, precision=lax.Precision.HIGHEST)).astype(
        jnp.bfloat16
    )
    return (next_gate, next_up, factor_gate, factor_up, resid_gate[None], resid_up[None])


def solution(mesh):
    finer = Mesh(
        mesh.devices.reshape(mesh.shape["outer"], 8, 8, 4), ("outer", "row_0", "row_1", "row_2")
    )
    placed = (P("outer", ROW, None), P("outer", ROW, None), P(None, ROW), P(None, ROW))
    return jax.shard_map(
        local,
        mesh=finer,
        in_specs=placed,
        out_specs=(
            P(None, ROW),
            P(None, ROW),
            P(ROW, None),
            P(ROW, None),
            P("outer", ROW, None),
            P("outer", ROW, None),
        ),
        check_vma=False,
    )
```

profile of v0, /device:TPU:1, one launch (start us, length us, event | category | flops | bytes accessed | tf_op | source)
XLA Modules:
  0.0 461.2 jit_solution(15747736612643531091)
XLA Ops:
  7.2 0.0 all-gather.2.cloned.1.call-start
  7.2 0.8 copy.45
  8.0 0.8 copy.44
  8.8 0.7 pad_maximum_fusion
  9.5 0.0 all-gather.2.cloned.1.call-update
  9.5 0.0 all-reduce.6.cloned.1.call-start
  9.6 0.0 copy-start
  9.6 131.7 %all-gather.2.cloned.1.call-done = bf16[14336,64]{1,0:T(8,128)(2,1)} async-done(((bf16[56,64]{1,0:T(8,128)(2,1)}), bf16[14336,64]{1,0:T(8,128)(2,1)}) %all-gather.2.cloned.1.call-update) | async-done | bytes 1835024 | tf_op jit(solution)/shard_map/all_gather | solution.py:15
  141.2 4.3 fusion.15
  145.6 0.1 copy.47
  145.6 0.1 reshape.80
  145.7 0.0 copy-done
  145.7 3.1 fusion.12
  148.9 0.1 copy.46
  149.0 0.1 reshape.79
  149.1 8.5 %all_to_all.6 = f32[2,1,2048]{2,1,0:T(1,128)S(1)} all-to-all(f32[2,1,2048]{2,1,0:T(1,128)S(1)} %broadcast_in_dim.7), channel_id=1, replica_groups=mesh['outer'=2,'row_0'=8,'row_1'=8,'row_2'=4] {'outer'}, dimensions={0} | all-to-all | bytes 32768 | tf_op jit(solution)/shard_map/all_to_all | solution.py:27
  157.6 0.1 convert_element_type.43
  157.7 1.7 fusion.21
  159.4 0.1 convert_element_type.45
  159.5 0.0 copy-done.1
  159.5 1.7 fusion.18
  161.2 0.0 all-reduce.6.cloned.1.call-update
  161.2 0.2 fusion.44
  161.4 0.2 fusion.45
  161.6 22.9 %all-reduce.2 = (f32[32,32]{0,1:T(8,128)S(1)}, f32[32,32]{0,1:T(8,128)S(1)}) all-reduce(f32[32,32]{0,1:T(8,128)S(1)} %fusion.44, f32[32,32]{0,1:T(8,128)S(1)} %fusion.45), channel_id=1, replica_groups=mesh['outer'=2,'row_0'=8,'row_1'=8,'row_2'=4] {'row_0'}, use_global_device_ids=true, to_apply=%region_1.0 | all-reduce | flops 2048 | bytes 16384 | tf_op jit(solution)/shard_map/psum | solution.py:46
  184.5 22.5 %all-reduce.1 = (f32[32,32]{0,1:T(8,128)S(1)}, f32[32,32]{0,1:T(8,128)S(1)}) all-reduce(f32[32,32]{0,1:T(8,128)S(1)} %get-tuple-element.43, f32[32,32]{0,1:T(8,128)S(1)} %get-tuple-element.44), channel_id=1, replica_groups=mesh['outer'=2,'row_0'=8,'row_1'=8,'row_2'=4] {'row_1'}, use_global_device_ids=true, to_apply=%region_2.0 | all-reduce | flops 2048 | bytes 16384 | tf_op jit(solution)/shard_map/psum | solution.py:46
  207.0 12.3 %all-reduce.3 = (f32[32,32]{0,1:T(8,128)S(1)}, f32[32,32]{0,1:T(8,128)S(1)}) all-reduce(f32[32,32]{0,1:T(8,128)S(1)} %get-tuple-element.41, f32[32,32]{0,1:T(8,128)S(1)} %get-tuple-element.42), channel_id=1, replica_groups=mesh['outer'=2,'row_0'=8,'row_1'=8,'row_2'=4] {'row_2'}, use_global_device_ids=true, to_apply=%region_3.0 | all-reduce | flops 2048 | bytes 16384 | tf_op jit(solution)/shard_map/psum | solution.py:46
  219.3 0.1 copy.52
  219.3 0.1 copy.50
  219.4 2.9 cholesky.44
  222.4 0.6 compare_reduce_fusion.1
  223.0 0.7 fusion.26
  223.7 2.4 custom-call.10
  226.1 2.9 cholesky.55
  229.1 0.6 compare_reduce_fusion
  229.7 0.7 fusion.27
  230.4 2.4 custom-call.11
  232.8 0.2 fusion.30
  233.0 0.7 copy.53
  233.7 0.2 fusion.28
  233.9 0.7 copy.54
  234.6 208.2 %all-reduce.6.cloned.1.call-done = (f32[32,14336]{1,0:T(8,128)}, f32[32,14336]{1,0:T(8,128)}) async-done(((f32[32,14336]{1,0:T(8,128)}, f32[32,14336]{1,0:T(8,128)}), (f32[32,14336]{1,0:T(8,128)}, f32[32,14336]{1,0:T(8,128)})) %all-reduce.6.cloned.1.call-update) | async-done | bytes 3670032 | tf_op jit(solution)/shard_map/psum | solution.py:86
  442.9 3.1 fusion.10
  446.0 2.7 fusion.3
  448.7 0.7 constant_dynamic-slice_fusion.1
  449.4 1.6 fusion.8
  451.0 0.7 constant_dynamic-slice_fusion
  451.7 2.6 fusion.2
  (10 shorter events, 0.1 us)
Async XLA Ops:
  7.2 134.1 %all-gather.2.cloned.1.call-start = ((), (), s32[]{:S(2)}) async-start(), calls=%async_computation.1 | async-start | bytes 3684352 | tf_op jit(solution)/shard_map/all_gather | solution.py:15
  9.5 433.4 %all-reduce.6.cloned.1.call-start = ((), (), s32[]{:S(2)}) async-start(), calls=%async_computation.2 | async-start | bytes 7340032 | tf_op jit(solution)/shard_map/psum | solution.py:86
  9.6 136.2 %copy-start = (bf16[1,32,14336]{2,1,0:T(8,128)(2,1)S(1)}, bf16[1,32,14336]{2,1,0:T(8,128)(2,1)}, u32[]{:S(2)}) copy-start(bf16[1,32,14336]{2,1,0:T(8,128)(2,1)} %param.9) | copy-start | bytes 2752516
  148.9 10.6 %copy-start.1 = (bf16[1,32,14336]{2,1,0:T(8,128)(2,1)S(1)}, bf16[1,32,14336]{2,1,0:T(8,128)(2,1)}, u32[]{:S(2)}) copy-start(bf16[1,32,14336]{2,1,0:T(8,128)(2,1)} %param.10) | copy-start | bytes 2752516
  446.0 3.3 copy-start.2
Sparse Core Ops, SparseCore 0:
  13.0 128.2 all-gather.1
  161.3 281.5 all-reduce.5
where the time goes:
time: 462 us; the launch traced here: 461 us
  waiting for transfers between devices  340 us (74%)
  blocking collectives  66.2 us (14%)
  matrix products  21.8 us (5%)
  other arithmetic  14.1 us (3%)
  between operations  14.1 us (3%)
  local copies, waits for them, and re-layouts  4.98 us (1%)
    psum x1, waiting for transfers between devices, local(): totals = lax.psum((products[0], products[1]), OUTER_ROW)  208 us
    all_gather x1, waiting for transfers between devices, gather_turned(): out = lax.all_gather(both, axis, axis=0, tiled=True)  132 us
    psum x3, blocking collectives, over_axes(): x = lax.psum(x, axis)  57.7 us
  transfers between devices with their start and end apart: 2, of which 2 were waited for; matrix products, arithmetic and copies ran while one was open for 3% of the time, Pallas kernels for 0%

commit v1 on v0

--- a/solution.py
+++ b/solution.py
@@ -12,7 +12,16 @@
     turned = [jnp.moveaxis(a, dim, 0) for a, dim in zip(arrays, dims)]
     widths = [t[0].size for t in turned]
     both = jnp.concatenate([t.reshape(-1, w) for t, w in zip(turned, widths)], axis=1)
-    out = lax.all_gather(both, axis, axis=0, tiled=True)
+    region_match = lambda body, group_axis: jnp.concatenate(
+        jax.lax.all_to_all(
+            jnp.stack([body for _ in range(jax.lax.axis_size(group_axis))]),
+            concat_axis=0,
+            split_axis=0,
+            axis_name=group_axis,
+        ),
+        0,
+    )
+    out = region_match(both, axis)
     tiles = jnp.split(out, [sum(widths[:k]) for k in range(1, len(widths))], axis=1)
     return tuple(
         (

time: 462 us -> 405 us (0.88)
  waiting for transfers between devices: 340 us -> 253 us
  starting transfers between devices: 0.08 us -> 23.2 us
  local copies, waits for them, and re-layouts: 4.98 us -> 16.3 us
    all_gather x1 -> x0, waiting for transfers between devices: 132 us -> none  [gather_turned(): out = lax.all_gather(both, axis, axis=0, tiled=True)]
    all_to_all x0 -> x1, waiting for transfers between devices: none -> 45.3 us  [gather_turned(): jax.lax.all_to_all(jnp.stack([body for _ in range(jax.lax.axis_size(group...]
    all_to_all x0 -> x1, starting transfers between devices: none -> 23.2 us  [gather_turned(): jax.lax.all_to_all(jnp.stack([body for _ in range(jax.lax.axis_size(group...]
    unnamed x10, local copies, waits for them, and re-layouts: 2.99 us -> 11.9 us
  transfers between devices with their start and end apart: 2 -> 2, of which waited for: 2 -> 2; matrix products, arithmetic and copies ran while one was open for 3% -> 4% of each run, Pallas kernels for 0% -> 0%
where the time goes in v1:
time: 405 us
  waiting for transfers between devices  253 us (62%)
  blocking collectives  62.5 us (15%)
  starting transfers between devices  23.2 us (6%)
  matrix products  21.6 us (5%)
  local copies, waits for them, and re-layouts  16.3 us (4%)
  between operations  14.2 us (4%)
  other arithmetic  14.1 us (3%)
    psum x1, waiting for transfers between devices, local(): totals = lax.psum((products[0], products[1]), OUTER_ROW)  207 us
    psum x3, blocking collectives, over_axes(): x = lax.psum(x, axis)  56.2 us
    all_to_all x1, waiting for transfers between devices, gather_turned(): jax.lax.all_to_all(jnp.stack([body for _ in range(jax.lax.axis_size(group...  45.3 us
    all_to_all x1, starting transfers between devices, gather_turned(): jax.lax.all_to_all(jnp.stack([body for _ in range(jax.lax.axis_size(group...  23.2 us
    unnamed x10, local copies, waits for them, and re-layouts  11.9 us
  transfers between devices with their start and end apart: 2, of which 2 were waited for; matrix products, arithmetic and copies ran while one was open for 4% of the time, Pallas kernels for 0%

profile of v1, /device:TPU:1, one launch (start us, length us, event | category | flops | bytes accessed | tf_op | source)
XLA Modules:
  0.0 404.5 jit_solution(5068107906102454936)
XLA Ops:
  7.2 0.7 pad_maximum_fusion
  7.9 0.1 copy.42
  8.0 2.3 stack.2
  10.3 6.9 %reshape.87 = bf16[256,2,1792]{2,1,0:T(2,128)(2,1)} reshape(bf16[256,56,64]{2,1,0:T(8,128)(2,1)} %stack.2) | data formatting | bytes 3670016
  17.1 23.2 %all-to-all-start = ((bf16[256,2,1792]{2,1,0:T(2,128)(2,1)}), bf16[256,2,1792]{2,1,0:T(2,128)(2,1)S(1)}, u32[]{:S(2)}, u32[]{:S(2)}) async-start(bf16[256,2,1792]{2,1,0:T(2,128)(2,1)} %reshape.87), calls=%async_computation | async-start | bytes 3670016 | tf_op jit(solution)/shard_map/all_to_all | solution.py:16
  40.3 0.0 all-reduce.6.cloned.1.call-start
  40.4 0.0 copy-start.1
  40.4 45.3 %all-to-all-done = bf16[256,2,1792]{2,1,0:T(2,128)(2,1)S(1)} async-done(((bf16[256,2,1792]{2,1,0:T(2,128)(2,1)}), bf16[256,2,1792]{2,1,0:T(2,128)(2,1)S(1)}, u32[]{:S(2)}, u32[]{:S(2)}) %all-to-all-start) | async-done | bytes 1835040 | tf_op jit(solution)/shard_map/all_to_all | solution.py:16
  85.7 3.6 reshape.88
  89.3 0.0 copy-done.1
  89.3 4.2 %fusion.15 = f32[32,32]{0,1:T(8,128)S(1)} fusion(bf16[14336,64]{1,0:T(8,128)(2,1)} %bitcast.67, bf16[1,32,14336]{2,1,0:T(8,128)(2,1)S(1)} %copy-done.1), kind=kOutput, calls=%fused_computation.15 | convolution fusion | flops 29360128 | bytes 2756608 | tf_op jit(solution)/shard_map/dot_general | solution.py:64
  93.4 0.1 copy.45
  93.5 0.1 reshape.86
  93.6 3.1 fusion.12
  96.7 0.1 copy.44
  96.8 0.1 reshape.85
  96.9 6.3 %all_to_all.11 = f32[2,1,2048]{2,1,0:T(1,128)S(1)} all-to-all(f32[2,1,2048]{2,1,0:T(1,128)S(1)} %broadcast_in_dim.7), channel_id=1, replica_groups=mesh['outer'=2,'row_0'=8,'row_1'=8,'row_2'=4] {'outer'}, dimensions={0} | all-to-all | bytes 32768 | tf_op jit(solution)/shard_map/all_to_all | solution.py:36
  103.3 0.1 convert_element_type.43
  103.4 1.7 fusion.21
  105.1 0.1 convert_element_type.45
  105.2 1.7 fusion.18
  106.9 0.0 all-reduce.6.cloned.1.call-update
  106.9 0.2 fusion.44
  107.1 0.2 fusion.45
  107.3 22.9 %all-reduce.2 = (f32[32,32]{0,1:T(8,128)S(1)}, f32[32,32]{0,1:T(8,128)S(1)}) all-reduce(f32[32,32]{0,1:T(8,128)S(1)} %fusion.44, f32[32,32]{0,1:T(8,128)S(1)} %fusion.45), channel_id=1, replica_groups=mesh['outer'=2,'row_0'=8,'row_1'=8,'row_2'=4] {'row_0'}, use_global_device_ids=true, to_apply=%region_1.0 | all-reduce | flops 2048 | bytes 16384 | tf_op jit(solution)/shard_map/psum | solution.py:55
  130.2 21.5 %all-reduce.1 = (f32[32,32]{0,1:T(8,128)S(1)}, f32[32,32]{0,1:T(8,128)S(1)}) all-reduce(f32[32,32]{0,1:T(8,128)S(1)} %get-tuple-element.43, f32[32,32]{0,1:T(8,128)S(1)} %get-tuple-element.44), channel_id=1, replica_groups=mesh['outer'=2,'row_0'=8,'row_1'=8,'row_2'=4] {'row_1'}, use_global_device_ids=true, to_apply=%region_2.0 | all-reduce | flops 2048 | bytes 16384 | tf_op jit(solution)/shard_map/psum | solution.py:55
  151.7 11.8 %all-reduce.3 = (f32[32,32]{0,1:T(8,128)S(1)}, f32[32,32]{0,1:T(8,128)S(1)}) all-reduce(f32[32,32]{0,1:T(8,128)S(1)} %get-tuple-element.41, f32[32,32]{0,1:T(8,128)S(1)} %get-tuple-element.42), channel_id=1, replica_groups=mesh['outer'=2,'row_0'=8,'row_1'=8,'row_2'=4] {'row_2'}, use_global_device_ids=true, to_apply=%region_3.0 | all-reduce | flops 2048 | bytes 16384 | tf_op jit(solution)/shard_map/psum | solution.py:55
  163.5 0.1 copy.50
  163.6 0.1 copy.48
  163.7 2.9 cholesky.44
  166.6 0.6 compare_reduce_fusion.1
  167.3 0.7 fusion.26
  167.9 2.4 custom-call.10
  170.4 2.9 cholesky.55
  173.3 0.6 compare_reduce_fusion
  174.0 0.7 fusion.27
  174.6 2.4 custom-call.11
  177.1 0.2 fusion.30
  177.3 0.7 copy.51
  178.0 0.2 fusion.28
  178.2 0.7 copy.52
  178.9 207.3 %all-reduce.6.cloned.1.call-done = (f32[32,14336]{1,0:T(8,128)}, f32[32,14336]{1,0:T(8,128)}) async-done(((f32[32,14336]{1,0:T(8,128)}, f32[32,14336]{1,0:T(8,128)}), (f32[32,14336]{1,0:T(8,128)}, f32[32,14336]{1,0:T(8,128)})) %all-reduce.6.cloned.1.call-update) | async-done | bytes 3670032 | tf_op jit(solution)/shard_map/psum | solution.py:95
  386.2 3.1 fusion.10
  389.3 2.7 fusion.3
  392.0 0.7 constant_dynamic-slice_fusion.1
  392.7 1.6 fusion.8
  394.3 0.7 constant_dynamic-slice_fusion
  395.0 2.6 fusion.2
  (11 shorter events, 0.1 us)
Async XLA Ops:
  17.1 68.5 %all-to-all-start = ((bf16[256,2,1792]{2,1,0:T(2,128)(2,1)}), bf16[256,2,1792]{2,1,0:T(2,128)(2,1)S(1)}, u32[]{:S(2)}, u32[]{:S(2)}) async-start(bf16[256,2,1792]{2,1,0:T(2,128)(2,1)} %reshape.87), calls=%async_computation | async-start | bytes 3670016 | tf_op jit(solution)/shard_map/all_to_all | solution.py:16
  40.3 345.9 %all-reduce.6.cloned.1.call-start = ((), (), s32[]{:S(2)}) async-start(), calls=%async_computation.2 | async-start | bytes 7340032 | tf_op jit(solution)/shard_map/psum | solution.py:95
  40.4 48.9 %copy-start.1 = (bf16[1,32,14336]{2,1,0:T(8,128)(2,1)S(1)}, bf16[1,32,14336]{2,1,0:T(8,128)(2,1)}, u32[]{:S(2)}) copy-start(bf16[1,32,14336]{2,1,0:T(8,128)(2,1)} %param.10) | copy-start | bytes 2752516
  89.3 4.3 %copy-start = (bf16[1,32,14336]{2,1,0:T(8,128)(2,1)S(1)}, bf16[1,32,14336]{2,1,0:T(8,128)(2,1)}, u32[]{:S(2)}) copy-start(bf16[1,32,14336]{2,1,0:T(8,128)(2,1)} %param.9) | copy-start | bytes 2752516
  389.3 3.3 copy-start.2
Sparse Core Ops, SparseCore 0:
  107.0 279.1 all-reduce.5

commit v2 on v0

--- a/solution.py
+++ b/solution.py
@@ -43,7 +43,8 @@
 
 def over_axes(x, axes):
     for axis in axes:
-        x = lax.psum(x, axis)
+        blocks = lax.all_gather(x, axis, axis=0, tiled=False)
+        x = blocks.sum(axis=0)
     return x
 
 

time: 462 us -> 525 us (1.14)
  blocking collectives: 66.2 us -> 101 us
  waiting for transfers between devices: 340 us -> 369 us
    all_gather x0 -> x6, blocking collectives: none -> 92.8 us  [over_axes(): blocks = lax.all_gather(x, axis, axis=0, tiled=False)]
    psum x3 -> x0, blocking collectives: 57.7 us -> none  [over_axes(): x = lax.psum(x, axis)]
    psum x1, waiting for transfers between devices: 208 us -> 238 us  [local(): totals = lax.psum((products[0], products[1]), OUTER_ROW)]
  transfers between devices with their start and end apart: 2 -> 2, of which waited for: 2 -> 2; matrix products, arithmetic and copies ran while one was open for 3% -> 2% of each run, Pallas kernels for 0% -> 0%
where the time goes in v2:
time: 525 us
  waiting for transfers between devices  369 us (70%)
  blocking collectives  101 us (19%)
  matrix products  22 us (4%)
  other arithmetic  14.2 us (3%)
  between operations  14.2 us (3%)
    psum x1, waiting for transfers between devices, local(): totals = lax.psum((products[0], products[1]), OUTER_ROW)  238 us
    all_gather x1, waiting for transfers between devices, gather_turned(): out = lax.all_gather(both, axis, axis=0, tiled=True)  132 us
    all_gather x6, blocking collectives, over_axes(): blocks = lax.all_gather(x, axis, axis=0, tiled=False)  92.8 us
  transfers between devices with their start and end apart: 2, of which 2 were waited for; matrix products, arithmetic and copies ran while one was open for 2% of the time, Pallas kernels for 0%

profile of v2, /device:TPU:1, one launch (start us, length us, event | category | flops | bytes accessed | tf_op | source)
XLA Modules:
  0.0 525.1 jit_solution(14257466853053223523)
XLA Ops:
  7.2 0.0 all-gather.8.cloned.1.call-start
  7.2 0.8 copy.37
  8.0 0.8 copy.36
  8.8 0.7 pad_maximum_fusion
  9.5 0.0 all-gather.8.cloned.1.call-update
  9.5 0.0 all-reduce.3.cloned.1.call-start
  9.6 0.0 copy-start
  9.6 131.7 %all-gather.8.cloned.1.call-done = bf16[14336,64]{1,0:T(8,128)(2,1)} async-done(((bf16[56,64]{1,0:T(8,128)(2,1)}), bf16[14336,64]{1,0:T(8,128)(2,1)}) %all-gather.8.cloned.1.call-update) | async-done | bytes 1835024 | tf_op jit(solution)/shard_map/all_gather | solution.py:15
  141.2 4.3 fusion.15
  145.6 0.1 copy.39
  145.6 0.1 reshape.80
  145.7 3.2 fusion.12
  149.0 0.1 copy.38
  149.0 0.1 reshape.79
  149.1 8.4 %all_to_all.6 = f32[2,1,2048]{2,1,0:T(1,128)S(1)} all-to-all(f32[2,1,2048]{2,1,0:T(1,128)S(1)} %broadcast_in_dim.7), channel_id=1, replica_groups=mesh['outer'=2,'row_0'=8,'row_1'=8,'row_2'=4] {'outer'}, dimensions={0} | all-to-all | bytes 32768 | tf_op jit(solution)/shard_map/all_to_all | solution.py:27
  157.6 0.1 convert_element_type.45
  157.7 1.7 fusion.18
  159.4 0.2 fusion.45
  159.6 0.1 convert_element_type.43
  159.6 1.7 fusion.21
  161.3 18.2 %all-gather.3 = f32[256,32]{1,0:T(8,128)S(1)} all-gather(f32[32,32]{1,0:T(8,128)S(1)} %fusion.45), channel_id=5, replica_groups=mesh['outer'=2,'row_0'=8,'row_1'=8,'row_2'=4] {'row_0'}, dimensions={0}, use_global_device_ids=true | all-gather | bytes 36864 | tf_op jit(solution)/shard_map/all_gather | solution.py:46
  179.6 18.2 %all-gather.4 = f32[256,32]{1,0:T(8,128)S(1)} all-gather(f32[32,32]{1,0:T(8,128)S(1)} %reduce_sum.67), channel_id=6, replica_groups=mesh['outer'=2,'row_0'=8,'row_1'=8,'row_2'=4] {'row_1'}, dimensions={0}, use_global_device_ids=true | all-gather | bytes 36864 | tf_op jit(solution)/shard_map/all_gather | solution.py:46
  197.8 9.0 %all-gather.5 = f32[128,32]{1,0:T(8,128)S(1)} all-gather(f32[32,32]{1,0:T(8,128)S(1)} %reduce_sum.68), channel_id=7, replica_groups=mesh['outer'=2,'row_0'=8,'row_1'=8,'row_2'=4] {'row_2'}, dimensions={0}, use_global_device_ids=true | all-gather | bytes 20480 | tf_op jit(solution)/shard_map/all_gather | solution.py:46
  206.8 0.1 copy.42
  206.9 2.9 cholesky.55
  209.8 0.0 all-reduce.3.cloned.1.call-update
  209.9 0.6 compare_reduce_fusion
  210.5 0.7 fusion.27
  211.2 2.4 custom-call.11
  213.6 0.2 fusion.44
  213.8 18.3 %all-gather = f32[256,32]{1,0:T(8,128)S(1)} all-gather(f32[32,32]{1,0:T(8,128)S(1)} %fusion.44), channel_id=2, replica_groups=mesh['outer'=2,'row_0'=8,'row_1'=8,'row_2'=4] {'row_0'}, dimensions={0}, use_global_device_ids=true | all-gather | bytes 36864 | tf_op jit(solution)/shard_map/all_gather | solution.py:46
  232.1 19.7 %all-gather.1 = f32[256,32]{1,0:T(8,128)S(1)} all-gather(f32[32,32]{1,0:T(8,128)S(1)} %reduce_sum.64), channel_id=3, replica_groups=mesh['outer'=2,'row_0'=8,'row_1'=8,'row_2'=4] {'row_1'}, dimensions={0}, use_global_device_ids=true | all-gather | bytes 36864 | tf_op jit(solution)/shard_map/all_gather | solution.py:46
  251.9 9.3 %all-gather.2 = f32[128,32]{1,0:T(8,128)S(1)} all-gather(f32[32,32]{1,0:T(8,128)S(1)} %reduce_sum.65), channel_id=4, replica_groups=mesh['outer'=2,'row_0'=8,'row_1'=8,'row_2'=4] {'row_2'}, dimensions={0}, use_global_device_ids=true | all-gather | bytes 20480 | tf_op jit(solution)/shard_map/all_gather | solution.py:46
  261.2 0.1 copy.41
  261.3 2.9 cholesky.44
  264.2 0.6 compare_reduce_fusion.1
  264.9 0.7 fusion.26
  265.5 2.4 custom-call.10
  268.0 0.2 fusion.30
  268.2 0.7 copy.43
  268.9 0.2 fusion.28
  269.1 0.7 copy.44
  269.8 237.5 %all-reduce.3.cloned.1.call-done = (f32[32,14336]{1,0:T(8,128)}, f32[32,14336]{1,0:T(8,128)}) async-done(((f32[32,14336]{1,0:T(8,128)}, f32[32,14336]{1,0:T(8,128)}), (f32[32,14336]{1,0:T(8,128)}, f32[32,14336]{1,0:T(8,128)})) %all-reduce.3.cloned.1.call-update) | async-done | bytes 3670032 | tf_op jit(solution)/shard_map/psum | solution.py:87
  507.3 3.3 fusion.8
  510.6 1.6 fusion.10
  512.3 2.7 fusion.3
  514.9 2.7 fusion.2
  517.6 0.7 constant_dynamic-slice_fusion
  (19 shorter events, 0.2 us)
Async XLA Ops:
  7.2 134.1 %all-gather.8.cloned.1.call-start = ((), (), s32[]{:S(2)}) async-start(), calls=%async_computation.1 | async-start | bytes 3684352 | tf_op jit(solution)/shard_map/all_gather | solution.py:15
  9.5 497.8 %all-reduce.3.cloned.1.call-start = ((), (), s32[]{:S(2)}) async-start(), calls=%async_computation.2 | async-start | bytes 7340032 | tf_op jit(solution)/shard_map/psum | solution.py:87
  9.6 136.2 %copy-start = (bf16[1,32,14336]{2,1,0:T(8,128)(2,1)S(1)}, bf16[1,32,14336]{2,1,0:T(8,128)(2,1)}, u32[]{:S(2)}) copy-start(bf16[1,32,14336]{2,1,0:T(8,128)(2,1)} %param.9) | copy-start | bytes 2752516
  145.7 11.9 %copy-start.1 = (bf16[1,32,14336]{2,1,0:T(8,128)(2,1)S(1)}, bf16[1,32,14336]{2,1,0:T(8,128)(2,1)}, u32[]{:S(2)}) copy-start(bf16[1,32,14336]{2,1,0:T(8,128)(2,1)} %param.10) | copy-start | bytes 2752516
  507.3 3.3 copy-start.2
Sparse Core Ops, SparseCore 0:
  13.0 128.2 all-gather.7
  210.0 297.3 all-reduce.2
